TPU v7x, 32 devices: a whole 2x2x4 slice. The times are simulated.
32 devices in a mesh: band: 2 (over x), img: 4 (over z), fsdp: 4 (over y, core).
Axes of the slice: x: 2, y: 2, z: 4, core: 2. Of those that a mesh axis runs over, the one named last changes fastest.
Arguments:
- block_input: bfloat16 [384, 14, 14, 512], P(('img', 'fsdp'), 'band'), may hold values from -6 to 6
- slot_used: int32 [16, 24], P(('img', 'fsdp')), may hold values from 0 to 1, as said below
- cotangent: bfloat16 [384, 14, 14, 512], P(('img', 'fsdp'), 'band'), may hold values from -6 to 6
- ln1_gain: bfloat16 [512], P('fsdp'), may hold values from 0.25 to 1.75
- ln1_bias: bfloat16 [512], P('fsdp'), may hold values from -3 to 3
- w_qkv: bfloat16 [512, 1536], P('fsdp')
- q_bias: bfloat16 [512], P('fsdp'), may hold values from -3 to 3
- v_bias: bfloat16 [512], P('fsdp'), may hold values from -3 to 3
- rel_table: bfloat16 [16, 169], P('fsdp'), may hold values from -4 to 4
- w_out: bfloat16 [512, 512], P('fsdp'), may hold values from -0.75 to 0.75
- out_bias: bfloat16 [512], P('fsdp'), may hold values from -3 to 3
- ln2_gain: bfloat16 [512], P('fsdp'), may hold values from 0.25 to 1.75
- ln2_bias: bfloat16 [512], P('fsdp'), may hold values from -3 to 3
- w_fc1: bfloat16 [512, 2048], P('fsdp'), may hold values from -0.25 to 0.25
- fc1_bias: bfloat16 [2048], P('fsdp'), may hold values from -3 to 3
- w_fc2: bfloat16 [2048, 512], P('fsdp'), may hold values from -0.125 to 0.125
- fc2_bias: bfloat16 [512], P('fsdp'), may hold values from -3 to 3
Outputs:
- block_output: bfloat16 [384, 14, 14, 512], P(('img', 'fsdp'), 'band')
- input_grad: float32 [384, 14, 14, 512], P(('img', 'fsdp'), 'band')
- ln1_gain_grad: float32 [512], P('fsdp')
- ln1_bias_grad: float32 [512], P('fsdp')
- w_qkv_grad: float32 [512, 1536], P('fsdp')
- q_bias_grad: float32 [512], P('fsdp')
- v_bias_grad: float32 [512], P('fsdp')
- rel_table_grad: float32 [16, 169], P('fsdp')
- w_out_grad: float32 [512, 512], P('fsdp')
- out_bias_grad: float32 [512], P('fsdp')
- ln2_gain_grad: float32 [512], P('fsdp')
- ln2_bias_grad: float32 [512], P('fsdp')
- w_fc1_grad: float32 [512, 2048], P('fsdp')
- fc1_bias_grad: float32 [2048], P('fsdp')
- w_fc2_grad: float32 [2048, 512], P('fsdp')
- fc2_bias_grad: float32 [512], P('fsdp')
Inputs may be any that keep to these rules, and one draw needn't show every extreme that they name: `slot_used`: each row holds between 16 and 24 ones in any positions; both counts occur in every draw.
All inputs are finite; a program needn't handle non-finite values.
Results may differ from a plain program's by a relative error of at most 0.013.
The roundings to bfloat16 on the way count: a program that leaves them out, or rounds other values in their place, can miss the bound.
Values may be sent and summed in bfloat16 or wider, within the bound.
No kernel may reach another device: no remote copies, remote signals or barrier semaphores. Data moves between devices by JAX's collectives and lax.ppermute only.
A program may use at most 320 MiB of HBM per device.

v0:
```python
import jax
import jax.numpy as jnp
from jax import lax
from jax.sharding import PartitionSpec as P

D = 512
HEADS = 16
WIN = 7
SHIFT = 3
SIDE = 14
TABLE = 169
EPSILON = 1e-05
NEGATIVE = -1e30


def from_partner(value, axis, apart):
    mask = 2**apart
    pairs = [(source, source ^ mask) for source in range(lax.axis_size(axis))]
    return lax.ppermute(value, axis, pairs)


def rel_onehot():
    length = WIN * WIN
    places = jnp.arange(length)
    rowpos = places // WIN
    colpos = places % WIN
    index = (rowpos[:, None] - rowpos[None, :] + WIN - 1) * (2 * WIN - 1) + (
        colpos[:, None] - colpos[None, :] + WIN - 1
    )
    return (index.reshape(-1)[:, None] == jnp.arange(TABLE)[None, :]).astype(jnp.float32)


def window_same():
    cells = jnp.arange(SIDE)
    region = jnp.where(cells < SIDE - WIN, 0, jnp.where(cells < SIDE - SHIFT, 1, 2))
    label = region[:, None] * 3 + region[None, :]
    per_image = SIDE // WIN
    label = (
        label.reshape(per_image, WIN, per_image, WIN).transpose(0, 2, 1, 3).reshape(-1, WIN * WIN)
    )
    return label[:, :, None] == label[:, None, :]


def normalize(values):
    center = values - jnp.mean(values, -1, keepdims=True)
    spread = jnp.mean(center * center, -1, keepdims=True)
    rstd = lax.rsqrt(spread + EPSILON)
    return (center * rstd, rstd)


def norm_back(grad_hat, normal, rstd):
    return rstd * (
        grad_hat
        - jnp.mean(grad_hat, -1, keepdims=True)
        - normal * jnp.mean(grad_hat * normal, -1, keepdims=True)
    )


def gelu_slope(pre):
    return (
        0.5 * (1.0 + lax.erf(pre * 0.7071067811865476))
        + pre * jnp.exp(-0.5 * pre * pre) * 0.3989422804014327
    )


def to_windows(tensor):
    count = tensor.shape[0]
    width = tensor.shape[-1]
    return (
        tensor.reshape(count, WIN, SIDE // WIN, WIN, width)
        .transpose(0, 2, 1, 3, 4)
        .reshape(-1, width)
    )


def from_windows(tensor, count):
    width = tensor.shape[-1]
    return (
        tensor.reshape(count, SIDE // WIN, WIN, WIN, width)
        .transpose(0, 2, 1, 3, 4)
        .reshape(count, WIN, SIDE, width)
    )


def attention_logits(queries, keys_win, bias, same):
    scores = jnp.einsum("wqhd,wkhd->whqk", queries, keys_win, preferred_element_type=jnp.float32)
    length = scores.shape[-1]
    scores = scores.reshape(-1, same.shape[0], HEADS, length, length) + bias[None, None]
    scores = jnp.where(same[None, :, None], scores, NEGATIVE)
    return scores.reshape(-1, HEADS, length, length)


def shards(
    block_input,
    slot_used,
    cotangent,
    ln1_gain,
    ln1_bias,
    w_qkv,
    q_bias,
    v_bias,
    rel_table,
    w_out,
    out_bias,
    ln2_gain,
    ln2_bias,
    w_fc1,
    fc1_bias,
    w_fc2,
    fc2_bias,
):
    f32 = jnp.float32
    bf16 = jnp.bfloat16
    (
        gain_low,
        beta_low,
        weight_qkv,
        qbias_low,
        vbias_low,
        table,
        weight_out,
        pbias_low,
        gain2_low,
        beta2_low,
        weight_up,
        ubias_low,
        weight_down,
        dbias_low,
    ) = (
        lax.all_gather(ln1_gain, "fsdp", axis=0, tiled=True),
        lax.all_gather(ln1_bias, "fsdp", axis=0, tiled=True),
        lax.all_gather(w_qkv, "fsdp", axis=0, tiled=True),
        lax.all_gather(q_bias, "fsdp", axis=0, tiled=True),
        lax.all_gather(v_bias, "fsdp", axis=0, tiled=True),
        lax.all_gather(rel_table, "fsdp", axis=0, tiled=True),
        lax.all_gather(w_out, "fsdp", axis=0, tiled=True),
        lax.all_gather(out_bias, "fsdp", axis=0, tiled=True),
        lax.all_gather(ln2_gain, "fsdp", axis=0, tiled=True),
        lax.all_gather(ln2_bias, "fsdp", axis=0, tiled=True),
        lax.all_gather(w_fc1, "fsdp", axis=0, tiled=True),
        lax.all_gather(fc1_bias, "fsdp", axis=0, tiled=True),
        lax.all_gather(w_fc2, "fsdp", axis=0, tiled=True),
        lax.all_gather(fc2_bias, "fsdp", axis=0, tiled=True),
    )
    gain_one = gain_low.astype(f32)
    beta_one = beta_low.astype(f32)
    query_bias = qbias_low.astype(f32)
    value_bias = vbias_low.astype(f32)
    proj_bias = pbias_low.astype(f32)
    gain_two = gain2_low.astype(f32)
    beta_two = beta2_low.astype(f32)
    up_bias = ubias_low.astype(f32)
    down_bias = dbias_low.astype(f32)
    slots = block_input.shape[0]
    length = WIN * WIN
    head_dim = D // HEADS
    scale = head_dim ** (-0.5)
    per_image = SIDE // WIN
    onehot = rel_onehot()
    bias = jnp.dot(table.astype(f32), onehot.T, precision=lax.Precision.HIGHEST).reshape(
        HEADS, length, length
    )
    same = lax.dynamic_slice_in_dim(window_same(), lax.axis_index("band") * per_image, per_image, 0)
    inputs = block_input.astype(f32).reshape(-1, D)
    hat_one, rstd_one = normalize(inputs)
    normed = (hat_one * gain_one + beta_one).astype(bf16).reshape(slots, WIN, SIDE, D)
    arrived = from_partner(normed[:, :SHIFT], "band", 0)
    shifted = jnp.roll(jnp.concatenate([normed[:, SHIFT:], arrived], axis=1), -SHIFT, axis=2)
    windows = to_windows(shifted)
    qkv = jnp.dot(windows, weight_qkv, preferred_element_type=f32)
    queries = ((qkv[:, :D] + query_bias) * scale).astype(bf16).reshape(-1, length, HEADS, head_dim)
    keys_win = qkv[:, D : 2 * D].astype(bf16).reshape(-1, length, HEADS, head_dim)
    values = (qkv[:, 2 * D :] + value_bias).astype(bf16).reshape(-1, length, HEADS, head_dim)
    scores = attention_logits(queries, keys_win, bias, same)
    peak = jnp.max(scores, -1, keepdims=True)
    lse = peak + jnp.log(jnp.sum(jnp.exp(scores - peak), -1, keepdims=True))
    probs = jnp.exp(scores - lse).astype(bf16)
    attended = (
        jnp.einsum("whqk,wkhd->wqhd", probs, values, preferred_element_type=f32)
        .astype(bf16)
        .reshape(-1, D)
    )
    proj = (jnp.dot(attended, weight_out, preferred_element_type=f32) + proj_bias).astype(bf16)
    framed = jnp.roll(from_windows(proj, slots), SHIFT, axis=2)
    returned = from_partner(framed[:, WIN - SHIFT :], "band", 0)
    restored = jnp.concatenate([returned, framed[:, : WIN - SHIFT]], axis=1)
    resid = inputs + restored.astype(f32).reshape(-1, D)
    hat_two, rstd_two = normalize(resid)
    normed_two = (hat_two * gain_two + beta_two).astype(bf16)
    pre = jnp.dot(normed_two, weight_up, preferred_element_type=f32) + up_bias
    act = jax.nn.gelu(pre, approximate=False).astype(bf16)
    mlp_out = jnp.dot(act, weight_down, preferred_element_type=f32) + down_bias
    used_rows = jnp.repeat(slot_used.reshape(-1).astype(f32), WIN * SIDE)[:, None]
    output = (used_rows * (resid + mlp_out)).astype(bf16)
    grad_out = cotangent.astype(f32).reshape(-1, D) * used_rows
    grad_low = grad_out.astype(bf16)
    grad_down = jnp.dot(act.T, grad_low, preferred_element_type=f32)
    grad_downb = jnp.sum(grad_out, 0)
    grad_pre = jnp.dot(grad_low, weight_down.T, preferred_element_type=f32) * gelu_slope(pre)
    grad_upb = jnp.sum(grad_pre, 0)
    grad_hidden = grad_pre.astype(bf16)
    grad_up = jnp.dot(normed_two.T, grad_hidden, preferred_element_type=f32)
    grad_normed_two = jnp.dot(grad_hidden, weight_up.T, preferred_element_type=f32)
    grad_gain_two = jnp.sum(grad_normed_two * hat_two, 0)
    grad_beta_two = jnp.sum(grad_normed_two, 0)
    grad_resid = grad_out + norm_back(grad_normed_two * gain_two, hat_two, rstd_two)
    grad_projb = jnp.sum(grad_resid, 0)
    resid_low = grad_resid.astype(bf16).reshape(slots, WIN, SIDE, D)
    crossed = from_partner(resid_low[:, :SHIFT], "band", 0)
    grad_proj = to_windows(
        jnp.roll(jnp.concatenate([resid_low[:, SHIFT:], crossed], axis=1), -SHIFT, axis=2)
    )
    grad_wout = jnp.dot(attended.T, grad_proj, preferred_element_type=f32)
    grad_attended = (
        jnp.dot(grad_proj, weight_out.T, preferred_element_type=f32)
        .astype(bf16)
        .reshape(-1, length, HEADS, head_dim)
    )
    recomputed = jnp.exp(attention_logits(queries, keys_win, bias, same) - lse)
    grad_probs = jnp.einsum("wqhd,wkhd->whqk", grad_attended, values, preferred_element_type=f32)
    grad_scores = recomputed * (grad_probs - jnp.sum(recomputed * grad_probs, -1, keepdims=True))
    grad_table = jnp.dot(
        jnp.sum(grad_scores, 0).reshape(HEADS, length * length),
        onehot,
        precision=lax.Precision.HIGHEST,
    )
    grad_logits = grad_scores.astype(bf16)
    grad_queries = (
        jnp.einsum("whqk,wkhd->wqhd", grad_logits, keys_win, preferred_element_type=f32).reshape(
            -1, D
        )
        * scale
    )
    grad_keys = jnp.einsum(
        "whqk,wqhd->wkhd", grad_logits, queries, preferred_element_type=f32
    ).reshape(-1, D)
    grad_values = jnp.einsum(
        "whqk,wqhd->wkhd", probs, grad_attended, preferred_element_type=f32
    ).reshape(-1, D)
    grad_qbias = jnp.sum(grad_queries, 0)
    grad_vbias = jnp.sum(grad_values, 0)
    grad_qkv = jnp.concatenate([grad_queries, grad_keys, grad_values], axis=1).astype(bf16)
    grad_wqkv = jnp.dot(windows.T, grad_qkv, preferred_element_type=f32)
    grad_shifted = jnp.dot(grad_qkv, weight_qkv.T, preferred_element_type=f32).astype(bf16)
    grad_framed = jnp.roll(from_windows(grad_shifted, slots), SHIFT, axis=2)
    grad_back = from_partner(grad_framed[:, WIN - SHIFT :], "band", 0)
    grad_normed = (
        jnp.concatenate([grad_back, grad_framed[:, : WIN - SHIFT]], axis=1)
        .astype(f32)
        .reshape(-1, D)
    )
    grad_gain_one = jnp.sum(grad_normed * hat_one, 0)
    grad_beta_one = jnp.sum(grad_normed, 0)
    grad_input = grad_resid + norm_back(grad_normed * gain_one, hat_one, rstd_one)
    final_output = output.reshape(slots, WIN, SIDE, D)
    final_grad = grad_input.reshape(slots, WIN, SIDE, D)
    s01, s02, s03, s04, s05, s06, s07, s08, s09, s10, s11, s12, s13, s14 = lax.psum(
        (
            grad_gain_one,
            grad_beta_one,
            grad_wqkv,
            grad_qbias,
            grad_vbias,
            grad_table,
            grad_wout,
            grad_projb,
            grad_gain_two,
            grad_beta_two,
            grad_up,
            grad_upb,
            grad_down,
            grad_downb,
        ),
        ("band", "img"),
    )
    r01, r02, r03, r04, r05, r06, r07, r08, r09, r10, r11, r12, r13, r14 = (
        lax.psum_scatter(s01, "fsdp", scatter_dimension=0, tiled=True),
        lax.psum_scatter(s02, "fsdp", scatter_dimension=0, tiled=True),
        lax.psum_scatter(s03, "fsdp", scatter_dimension=0, tiled=True),
        lax.psum_scatter(s04, "fsdp", scatter_dimension=0, tiled=True),
        lax.psum_scatter(s05, "fsdp", scatter_dimension=0, tiled=True),
        lax.psum_scatter(s06, "fsdp", scatter_dimension=0, tiled=True),
        lax.psum_scatter(s07, "fsdp", scatter_dimension=0, tiled=True),
        lax.psum_scatter(s08, "fsdp", scatter_dimension=0, tiled=True),
        lax.psum_scatter(s09, "fsdp", scatter_dimension=0, tiled=True),
        lax.psum_scatter(s10, "fsdp", scatter_dimension=0, tiled=True),
        lax.psum_scatter(s11, "fsdp", scatter_dimension=0, tiled=True),
        lax.psum_scatter(s12, "fsdp", scatter_dimension=0, tiled=True),
        lax.psum_scatter(s13, "fsdp", scatter_dimension=0, tiled=True),
        lax.psum_scatter(s14, "fsdp", scatter_dimension=0, tiled=True),
    )
    return (
        final_output,
        final_grad,
        r01,
        r02,
        r03,
        r04,
        r05,
        r06,
        r07,
        r08,
        r09,
        r10,
        r11,
        r12,
        r13,
        r14,
    )


def solution(mesh):
    placed = (
        P(("img", "fsdp"), "band", None, None),
        P(("img", "fsdp"), None),
        P(("img", "fsdp"), "band", None, None),
        P("fsdp"),
        P("fsdp"),
        P("fsdp", None),
        P("fsdp"),
        P("fsdp"),
        P("fsdp", None),
        P("fsdp", None),
        P("fsdp"),
        P("fsdp"),
        P("fsdp"),
        P("fsdp", None),
        P("fsdp"),
        P("fsdp", None),
        P("fsdp"),
    )
    return jax.shard_map(
        shards,
        mesh=mesh,
        in_specs=placed,
        out_specs=(
            P(("img", "fsdp"), "band", None, None),
            P(("img", "fsdp"), "band", None, None),
            P("fsdp"),
            P("fsdp"),
            P("fsdp", None),
            P("fsdp"),
            P("fsdp"),
            P("fsdp", None),
            P("fsdp", None),
            P("fsdp"),
            P("fsdp"),
            P("fsdp"),
            P("fsdp", None),
            P("fsdp"),
            P("fsdp", None),
            P("fsdp"),
        ),
        check_vma=False,
    )
```

profile of v0, /device:TPU:0, one launch (start us, length us, event | category | flops | bytes accessed | tf_op | source)
XLA Modules:
  0.0 890.9 jit_solution(15372807008228085413)
XLA Ops:
  8.0 6.2 all-gather
  54.8 7.9 all_gather.48
  73.1 6.2 fusion.53
  84.7 11.5 %reshape.462 = bf16[48,49,16,32]{3,2,1,0:T(8,128)(2,1)} reshape(bf16[2352,512]{1,0:T(8,128)(2,1)} %get-tuple-element.117) | data formatting | bytes 4816896 | tf_op jit(solution)/shard_map/reshape | solution.py:171
  96.2 13.5 %copy.127 = bf16[48,49,16,32]{1,3,2,0:T(8,128)(2,1)} copy(bf16[48,49,16,32]{3,2,1,0:T(8,128)(2,1)} %reshape.462) | data formatting | bytes 4816896 | tf_op jit(solution)/shard_map/reshape | solution.py:171
  109.8 11.5 %reshape.463 = bf16[48,49,16,32]{3,2,1,0:T(8,128)(2,1)} reshape(bf16[2352,512]{1,0:T(8,128)(2,1)} %slice.113) | data formatting | bytes 4816896 | tf_op jit(solution)/shard_map/reshape | solution.py:172
  121.3 13.5 %copy.128 = bf16[48,49,16,32]{1,3,2,0:T(8,128)(2,1)} copy(bf16[48,49,16,32]{3,2,1,0:T(8,128)(2,1)} %reshape.463) | data formatting | bytes 4816896 | tf_op jit(solution)/shard_map/reshape | solution.py:172
  134.9 13.4 %fusion.15 = (f32[48,16,49]{2,1,0:T(8,128)S(1)}, f32[48,16,49,49]{2,3,1,0:T(8,128)}) fusion(f32[16,49,49]{1,2,0:T(8,128)S(1)} %copy.129, pred[48,49,49]{1,2,0:T(8,128)(4,1)S(1)} %bitcast.95, bf16[48,49,16,32]{1,3,2,0:T(8,128)(2,1)} %copy.127, bf16[48,49,16,32]{1,3,2,0:T(8,128)(2,1)} %copy.128), kind=kOutput, calls=%fused_computation.30 | convolution fusion | flops 123508224 | bytes 12612208 | tf_op jit(solution)/shard_map/wqhd,wkhd->whqk/dot_general | solution.py:86
  148.3 13.4 %exponential_reduce_fusion = f32[48,16,49]{2,1,0:T(8,128)S(1)} fusion(f32[48,16,49,49]{2,3,1,0:T(8,128)} %get-tuple-element.122, f32[48,16,49]{2,1,0:T(8,128)S(1)} %get-tuple-element.121, f32[16,49,49]{1,2,0:T(8,128)S(1)} %copy.129, pred[48,49,49]{1,2,0:T(8,128)(4,1)S(1)} %bitcast.96), kind=kLoop, calls=%fused_computation.5 | loop fusion | flops 7338240 | bytes 7945840 | tf_op jit(solution)/shard_map/reduce_sum | solution.py:176
  162.5 11.5 %reshape.461 = bf16[48,49,16,32]{3,2,1,0:T(8,128)(2,1)} reshape(bf16[2352,512]{1,0:T(8,128)(2,1)} %get-tuple-element.118) | data formatting | bytes 4816896 | tf_op jit(solution)/shard_map/reshape | solution.py:173
  174.0 13.5 %copy.130 = bf16[48,49,16,32]{1,3,2,0:T(8,128)(2,1)} copy(bf16[48,49,16,32]{3,2,1,0:T(8,128)(2,1)} %reshape.461) | data formatting | bytes 4816896 | tf_op jit(solution)/shard_map/reshape | solution.py:173
  187.6 14.4 %convert_bitcast_fusion.1 = bf16[48,49,16,32]{1,3,2,0:T(8,128)(2,1)} fusion(bf16[48,49,16,32]{1,3,2,0:T(8,128)(2,1)} %copy.130, f32[48,16,49,49]{2,3,1,0:T(8,128)} %get-tuple-element.122, f32[48,16,49]{2,1,0:T(8,128)} %log_add_fusion, f32[16,49,49]{1,2,0:T(8,128)S(1)} %copy.129, pred[48,49,49]{1,2,0:T(8,128)(4,1)S(1)} %bitcast.97), kind=kOutput, calls=%fused_computation.38 | convolution fusion | flops 126594048 | bytes 12612208 | tf_op jit(solution)/shard_map/whqk,wkhd->wqhd/dot_general | solution.py:179
  201.9 9.5 %copy.132 = bf16[48,49,16,32]{1,0,3,2:T(8,128)(2,1)} copy(bf16[48,49,16,32]{1,3,2,0:T(8,128)(2,1)} %convert_bitcast_fusion.1) | data formatting | bytes 4816896 | tf_op jit(solution)/shard_map/convert_element_type | solution.py:180
  211.5 9.2 %reshape.405 = bf16[2352,512]{0,1:T(8,128)(2,1)} reshape(bf16[48,49,16,32]{1,0,3,2:T(8,128)(2,1)} %copy.132) | data formatting | bytes 4816896 | tf_op jit(solution)/shard_map/reshape | solution.py:181
  261.2 6.3 reshape.409
  267.6 6.3 reshape.399
  286.5 6.4 reshape.420
  292.9 7.1 add.283
  300.0 49.9 %fusion.2 = (bf16[2352,2048]{1,0:T(8,128)(2,1)}, f32[2352,2048]{1,0:T(8,128)}) fusion(f32[2048]{0:T(1024)S(1)} %bitcast.122, bf16[512,2048]{1,0:T(8,128)(2,1)} %all-gather.16.cloned.1.call-done, f32[2352,512]{1,0:T(8,128)} %add.283, f32[512]{0:T(512)S(1)} %bitcast.125, f32[512]{0:T(512)S(1)} %bitcast.115, f32[2352]{0:T(1024)S(1)} %rsqrt.25, f32[2352]{0:T(1024)S(1)} %div.52), kind=kOutput, calls=%fused_computation.9 | convolution fusion | flops 5256437760 | bytes 35846528 | tf_op jit(solution)/shard_map/dot_general | solution.py:190
  349.9 18.1 %fusion.50 = (f32[2048]{0:T(1024)}, bf16[2352,2048]{1,0:T(8,128)(2,1)}) fusion(f32[2352,2048]{1,0:T(8,128)} %get-tuple-element.124, f32[2048]{0:T(1024)S(1)} %bitcast.123, bf16[2048,512]{1,0:T(8,128)(2,1)} %all-gather.18.cloned.1.call-done, f32[2352,512]{1,0:T(8,128)} %reshape.409, f32[2352]{0:T(1024)S(1)} %copy-done.31), kind=kOutput, calls=%fused_computation.130 | convolution fusion | flops 4992710656 | bytes 35841216 | tf_op jit(solution)/shard_map/dot_general | solution.py:199
  368.0 12.3 %multiply_reduce_fusion.3 = (f32[512]{0:T(512)}, f32[2352]{0:T(1024)S(1)}, f32[2352]{0:T(1024)S(1)}, f32[512]{0:T(512)}, f32[2352,512]{1,0:T(8,128)S(1)}) fusion(f32[2352,512]{1,0:T(8,128)S(1)} %copy-done.9, f32[2352]{0:T(1024)S(1)} %rsqrt.25, f32[2352]{0:T(1024)S(1)} %div.52, f32[512]{0:T(512)S(1)} %bitcast.116, bf16[512,2048]{1,0:T(8,128)(2,1)S(1)} %copy-done.56, ...), kind=kOutput, calls=%fused_computation.51 | convolution fusion | flops 4943333376 | bytes 21408512 | tf_op jit(solution)/shard_map/dot_general | solution.py:203
  393.5 23.3 %collective-permute-done.2 = bf16[24,3,14,512]{3,0,2,1:T(8,128)(2,1)S(1)} collective-permute-done((bf16[24,3,14,512]{3,0,2,1:T(8,128)(2,1)S(1)}, bf16[24,3,14,512]{3,0,2,1:T(8,128)(2,1)S(1)}, u32[]{:S(2)}, u32[]{:S(2)}) %collective-permute-start.2) | collective-permute-done | bytes 1032224 | tf_op jit(solution)/shard_map/ppermute | solution.py:19
  431.4 11.5 %reshape.464 = bf16[48,49,16,32]{3,2,1,0:T(8,128)(2,1)} reshape(bf16[2352,512]{1,0:T(8,128)(2,1)} %convolution_convert_fusion.1) | data formatting | bytes 4816896 | tf_op jit(solution)/shard_map/reshape | solution.py:217
  442.9 13.6 %copy.144 = bf16[48,49,16,32]{1,3,2,0:T(8,128)(2,1)} copy(bf16[48,49,16,32]{3,2,1,0:T(8,128)(2,1)} %reshape.464) | data formatting | bytes 4816896 | tf_op jit(solution)/shard_map/reshape | solution.py:217
  456.6 23.3 %multiply_reduce_fusion = (f32[48,16,49]{2,1,0:T(8,128)S(1)}, f32[48,16,49,49]{2,3,1,0:T(8,128)}) fusion(f32[48,16,49,49]{2,3,1,0:T(8,128)} %get-tuple-element.122, f32[48,16,49]{2,1,0:T(8,128)S(1)} %copy-done.8, f32[16,49,49]{1,2,0:T(8,128)S(1)} %copy-done.3, pred[48,49,49]{1,2,0:T(8,128)(4,1)S(1)} %bitcast.98, bf16[48,49,16,32]{1,3,2,0:T(8,128)(2,1)} %copy.144, ...), kind=kOutput, calls=%fused_computation.3 | convolution fusion | flops 127196160 | bytes 20138608 | tf_op jit(solution)/shard_map/wqhd,wkhd->whqk/dot_general | solution.py:220
  479.9 19.4 %bitcast_convert_fusion = (bf16[48,49,16,32]{1,3,2,0:T(8,128)(2,1)}, f32[48,16,32,49]{3,2,1,0:T(8,128)}) fusion(bf16[48,49,16,32]{1,3,2,0:T(8,128)(2,1)} %copy.144, f32[48,16,49,49]{2,3,1,0:T(8,128)} %get-tuple-element.122, f32[48,16,49]{2,1,0:T(8,128)S(1)} %copy-done.8, f32[16,49,49]{1,2,0:T(8,128)S(1)} %copy-done.3, pred[48,49,49]{1,2,0:T(8,128)(4,1)S(1)} %bitcast.99), kind=kOutput, calls=%fused_computation.32 | convolution fusion | flops 126594048 | bytes 17429104 | tf_op jit(solution)/shard_map/whqk,wqhd->wkhd/dot_general | solution.py:237
  499.2 21.2 %fusion.48 = (f32[16,49,49]{1,2,0:T(8,128)}, bf16[48,16,49,49]{2,3,1,0:T(8,128)(2,1)}) fusion(f32[48,16,49,49]{2,3,1,0:T(8,128)} %get-tuple-element.127, f32[48,16,49]{2,1,0:T(8,128)S(1)} %get-tuple-element.126, f32[48,16,49]{2,1,0:T(8,128)S(1)} %copy-done.8, f32[48,16,49,49]{2,3,1,0:T(8,128)} %get-tuple-element.122, f32[16,49,49]{1,2,0:T(8,128)S(1)} %copy-done.3, ...), kind=kLoop, calls=%fused_computation.129 | loop fusion | flops 12869360 | bytes 19163312 | tf_op jit(solution)/shard_map/reduce_sum | solution.py:223
  520.4 10.4 %convert_bitcast_fusion = bf16[48,49,16,32]{1,3,2,0:T(8,128)(2,1)} fusion(bf16[48,49,16,32]{1,3,2,0:T(8,128)(2,1)S(1)} %bitcast.94, bf16[48,16,49,49]{2,3,1,0:T(8,128)(2,1)} %get-tuple-element.115), kind=kOutput, calls=%fused_computation.37 | convolution fusion | flops 119218176 | bytes 8504832 | tf_op jit(solution)/shard_map/whqk,wqhd->wkhd/dot_general | solution.py:234
  530.8 11.9 %multiply_reduce_fusion.1 = (f32[16,32]{1,0:T(8,128)S(1)}, bf16[48,49,16,32]{1,3,2,0:T(8,128)(2,1)}) fusion(bf16[48,49,16,32]{1,3,2,0:T(8,128)(2,1)} %copy.128, bf16[48,16,49,49]{2,3,1,0:T(8,128)(2,1)} %get-tuple-element.115), kind=kOutput, calls=%fused_computation.33 | convolution fusion | flops 121626112 | bytes 8506880 | tf_op jit(solution)/shard_map/whqk,wkhd->wqhd/dot_general | solution.py:229
  542.8 9.6 %copy.151 = bf16[48,49,16,32]{1,0,3,2:T(8,128)(2,1)} copy(bf16[48,49,16,32]{1,3,2,0:T(8,128)(2,1)} %convert_bitcast_fusion) | data formatting | bytes 4816896 | tf_op jit(solution)/shard_map/whqk,wqhd->wkhd/transpose | solution.py:234
  552.3 8.5 reshape.414
  560.8 9.6 %copy.154 = bf16[48,49,16,32]{1,0,3,2:T(8,128)(2,1)} copy(bf16[48,49,16,32]{1,3,2,0:T(8,128)(2,1)} %get-tuple-element.128) | data formatting | bytes 4816896 | tf_op jit(solution)/shard_map/convert.5
  570.4 9.2 %reshape.415 = bf16[2352,512]{0,1:T(8,128)(2,1)} reshape(bf16[48,49,16,32]{1,0,3,2:T(8,128)(2,1)} %copy.154) | data formatting | bytes 4816896 | tf_op jit(solution)/shard_map/reshape | solution.py:239
  579.6 9.4 %copy.148 = bf16[48,49,16,32]{1,0,3,2:T(8,128)(2,1)} copy(bf16[48,49,16,32]{1,3,2,0:T(8,128)(2,1)} %get-tuple-element.120) | data formatting | bytes 4816896 | tf_op jit(solution)/shard_map/mul | solution.py:229
  589.0 9.3 %mul.250 = bf16[2352,512]{0,1:T(8,128)(2,1)} reshape(bf16[48,49,16,32]{1,0,3,2:T(8,128)(2,1)} %copy.148) | data formatting | bytes 4816896 | tf_op jit(solution)/shard_map/mul | solution.py:229
  610.2 11.0 %fusion.42 = f32[2048,512]{1,0:T(8,128)} fusion(bf16[2352,2048]{1,0:T(8,128)(2,1)} %get-tuple-element.123, f32[2352,512]{1,0:T(8,128)} %reshape.409, f32[2352]{0:T(1024)S(1)} %copy-done.32), kind=kOutput, calls=%fused_computation.125 | convolution fusion | flops 4934909952 | bytes 18654400 | tf_op jit(solution)/shard_map/dot_general | solution.py:197
  621.6 13.1 %fusion.25 = f32[512,2048]{1,0:T(8,128)} fusion(bf16[2352,2048]{1,0:T(8,128)(2,1)} %get-tuple-element.131, f32[2352,512]{1,0:T(8,128)} %add.283, f32[512]{0:T(512)S(1)} %bitcast.126, f32[512]{0:T(512)S(1)} %bitcast.118, f32[2352]{0:T(1024)S(1)} %copy-done.28, f32[2352]{0:T(1024)S(1)} %copy-done.30), kind=kOutput, calls=%fused_computation.57 | convolution fusion | flops 4938522624 | bytes 18667904 | tf_op jit(solution)/shard_map/dot_general | solution.py:202
  644.0 9.3 %convolution_convert_fusion = bf16[2352,512]{1,0:T(8,128)(2,1)} fusion(bf16[2352,1536]{0,1:T(8,128)(2,1)} %copy-done.23, bf16[512,1536]{1,0:T(8,128)(2,1)} %all-gather.14.cloned.1.call-done), kind=kOutput, calls=%fused_computation.74 | convolution fusion | flops 3700580352 | bytes 11206656 | tf_op jit(solution)/shard_map/dot_general | solution.py:244
  662.7 10.6 %multiply_convert_fusion.1 = bf16[2352,512]{1,0:T(8,128)(2,1)} fusion(f32[2352,512]{1,0:T(8,128)S(1)} %bitcast.102, bf16[2352,2048]{1,0:T(8,128)(2,1)} %get-tuple-element.123, bf16[2048,512]{1,0:T(8,128)(2,1)S(1)} %copy-done.55, f32[512]{0:T(512)S(1)} %bitcast.128, f32[2352]{0:T(1024)S(1)} %copy-done.32), kind=kOutput, calls=%fused_computation.61 | convolution fusion | flops 4937318400 | bytes 18967744 | tf_op jit(solution)/shard_map/dot_general | solution.py:192
  681.2 15.3 %reduce-scatter.11.cloned.1.call-done = f32[512,512]{1,0:T(8,128)} async-done(((f32[2048,512]{1,0:T(8,128)}), f32[512,512]{1,0:T(8,128)}) %reduce-scatter.11.cloned.1.call-update) | async-done | bytes 1048592 | tf_op jit(solution)/shard_map/reduce_scatter | solution.py:289
  696.5 47.1 %reduce-scatter.9.cloned.1.call-done = f32[128,2048]{1,0:T(8,128)} async-done(((f32[512,2048]{1,0:T(8,128)}), f32[128,2048]{1,0:T(8,128)}) %reduce-scatter.9.cloned.1.call-update) | async-done | bytes 1048592 | tf_op jit(solution)/shard_map/reduce_scatter | solution.py:287
  755.9 11.6 %all-reduce.12 = (f32[512]{0:T(512)S(1)}, f32[512]{0:T(512)S(1)}, f32[512]{0:T(512)S(1)}, f32[512]{0:T(512)S(1)}, f32[16,169]{1,0:T(8,128)S(1)}, /*index=5*/f32[...) all-reduce(f32[512]{0:T(512)S(1)} %get-tuple-element.82, ...), channel_id=2, replica_groups=mesh['band'=2,'img'=4,'fsdp'=4] {'fsdp'}, use_global_device_ids=true, to_apply=%region_13.14.clone | all-reduce | flops 8848 | bytes 70784
  773.6 6.4 reshape.421
  780.1 8.1 multiply_add_fusion
  788.2 6.3 reshape.418
  794.4 7.8 copy.162
  802.3 37.5 %all-reduce.10 = (f32[128]{0:T(128)}, f32[128]{0:T(128)}, f32[128]{0:T(128)}, f32[128]{0:T(128)}, f32[4,169]{1,0:T(4,128)}, /*index=5*/f32[128]{0:T(128)}, f32[1...) all-reduce(f32[128]{0:T(128)S(1)} %dynamic-slice.1, ...), channel_id=1, replica_groups=mesh['band'=2,'img'=4,'fsdp'=4] {'band','img'}, use_global_device_ids=true, to_apply=%region_12.13 | all-reduce | flops 2212 | bytes 17696 | tf_op jit(solution)/shard_map/psum | solution.py:257
  839.8 36.6 %all-reduce.15.cloned.1.call-done = (f32[128,1536]{1,0:T(8,128)}, f32[128,512]{1,0:T(8,128)}, f32[128,2048]{1,0:T(8,128)}, f32[512,512]{1,0:T(8,128)}) async-done(((f32[128,1536]{1,0:T(8,128)}, f32[128,512]{1,0:T(8,128)}, f32[128,2048]{1,0:T(8,128)}, f32[512,512]{1,0:T(8,128)}), (f32[128,1536]{1,0:T(8,128)}, f32[128,512]{1,0:T(8,128)}, f32[128,2048]{1,0:T(8,128)}, ...) | async-done | bytes 3145744 | tf_op jit(solution)/shard_map/psum | solution.py:257
  (284 shorter events, 200.8 us)
Async XLA Ops:
  7.2 17.4 %copy-start = (bf16[24,7,14,512]{3,0,2,1:T(8,128)(2,1)S(1)}, bf16[24,7,14,512]{3,0,2,1:T(8,128)(2,1)}, u32[]{:S(2)}) copy-start(bf16[24,7,14,512]{3,0,2,1:T(8,128)(2,1)} %param.17) | copy-start | bytes 7225348
  7.2 65.9 %all-gather.14.cloned.1.call-start = ((), (), s32[]{:S(2)}) async-start(), calls=%async_computation.4 | async-start | bytes 1966080 | tf_op jit(solution)/shard_map/all_gather | solution.py:132
  7.9 292.1 %all-gather.16.cloned.1.call-start = ((), (), s32[]{:S(2)}) async-start(), calls=%async_computation.5 | async-start | bytes 2621440 | tf_op jit(solution)/shard_map/all_gather | solution.py:140
  14.2 11.5 %copy-start.33 = (f32[4,1,128]{2,1,0:T(1,128)}, f32[4,1,128]{2,1,0:T(1,128)S(1)}, u32[]{:S(2)}) copy-start(f32[4,1,128]{2,1,0:T(1,128)S(1)} %convert_element_type.153) | copy-start | bytes 6148
  24.6 13.1 %copy-start.50 = (bf16[128]{0:T(256)(128)(2,1)S(1)}, bf16[128]{0:T(256)(128)(2,1)}, u32[]{:S(2)}) copy-start(bf16[128]{0:T(256)(128)(2,1)} %param.24) | copy-start | bytes 772
  24.7 18.1 %copy-start.51 = (bf16[128]{0:T(256)(128)(2,1)S(1)}, bf16[128]{0:T(256)(128)(2,1)}, u32[]{:S(2)}) copy-start(bf16[128]{0:T(256)(128)(2,1)} %param.27) | copy-start | bytes 772
  24.7 23.3 %copy-start.43 = (bf16[4,169]{1,0:T(4,128)(2,1)S(1)}, bf16[4,169]{1,0:T(4,128)(2,1)}, u32[]{:S(2)}) copy-start(bf16[4,169]{1,0:T(4,128)(2,1)} %param.25) | copy-start | bytes 4060
  27.2 27.6 %copy-start.26 = (bf16[128,512]{1,0:T(8,128)(2,1)S(1)}, bf16[128,512]{1,0:T(8,128)(2,1)}, u32[]{:S(2)}) copy-start(bf16[128,512]{1,0:T(8,128)(2,1)} %param.26) | copy-start | bytes 393220
  28.2 34.5 %collective-permute-start = (bf16[24,3,14,512]{3,0,2,1:T(8,128)(2,1)}, bf16[24,3,14,512]{3,0,2,1:T(8,128)(2,1)}, u32[]{:S(2)}, u32[]{:S(2)}) collective-permute-start(bf16[24,3,14,512]{3,0,2,1:T(8,128)(2,1)} %slice.82), channel_id=1, source_target_pairs={{0,16},{16,0},{1,17},{17,1},{2,18},{18,2},{3,19},{19,3},{4,20},{20... | collective-permute-start | bytes 3096584 | tf_op jit(solution)/shard_map/ppermute | solution.py:19
  30.0 319.9 %all-gather.18.cloned.1.call-start = ((), (), s32[]{:S(2)}) async-start(), calls=%async_computation.6 | async-start | bytes 2621440 | tf_op jit(solution)/shard_map/all_gather | solution.py:142
  54.7 132.9 %copy-start.2 = (f32[16,49,49]{1,2,0:T(8,128)}, f32[16,49,49]{1,2,0:T(8,128)S(1)}, u32[]{:S(2)}) copy-start(f32[16,49,49]{1,2,0:T(8,128)S(1)} %copy.129) | copy-start | bytes 460996
  54.7 9.6 %copy-start.12 = (bf16[24,4,14,512]{3,0,2,1:T(8,128)(2,1)S(1)}, bf16[24,4,14,512]{3,0,2,1:T(8,128)(2,1)}, u32[]{:S(2)}) copy-start(bf16[24,4,14,512]{3,0,2,1:T(8,128)(2,1)} %slice.81) | copy-start | bytes 4128772
  134.9 52.7 %copy-start.6 = (pred[24,2,49,49]{2,3,1,0:T(8,128)(4,1)}, pred[24,2,49,49]{2,3,1,0:T(8,128)(4,1)S(1)}, u32[]{:S(2)}) copy-start(pred[24,2,49,49]{2,3,1,0:T(8,128)(4,1)S(1)} %broadcast_in_dim.38) | copy-start | bytes 345748
  211.5 9.2 %copy-start.24 = (bf16[512,512]{1,0:T(8,128)(2,1)S(1)}, bf16[512,512]{1,0:T(8,128)(2,1)}, u32[]{:S(2)}) copy-start(bf16[512,512]{1,0:T(8,128)(2,1)} %all_gather.48) | copy-start | bytes 1572868
  236.1 14.0 %copy-start.48 = (bf16[512]{0:T(512)(128)(2,1)S(1)}, bf16[512]{0:T(512)(128)(2,1)}, u32[]{:S(2)}) copy-start(bf16[512]{0:T(512)(128)(2,1)} %param.31) | copy-start | bytes 3076
  236.1 19.5 %copy-start.57 = (s32[1,24]{1,0:T(1,128)S(1)}, s32[1,24]{1,0:T(1,128)}, u32[]{:S(2)}) copy-start(s32[1,24]{1,0:T(1,128)} %param.18) | copy-start | bytes 292
  236.1 37.8 %collective-permute-start.1 = (bf16[24,3,14,512]{3,0,2,1:T(8,128)(2,1)}, bf16[24,3,14,512]{3,0,2,1:T(8,128)(2,1)}, u32[]{:S(2)}, u32[]{:S(2)}) collective-permute-start(bf16[24,3,14,512]{3,0,2,1:T(8,128)(2,1)} %pad_maximum_fusion.5), channel_id=1, source_target_pairs={{0,16},{16,0},{1,17},{17,1},{2,18},{18,2},{3,19},{19,3},{4,20},{20... | collective-permute-start | bytes 3096584 | tf_op jit(solution)/shard_map/ppermute | solution.py:19
  236.6 444.6 %reduce-scatter.7.cloned.1.call-start = ((), (), s32[]{:S(2)}) async-start(), calls=%async_computation.8 | async-start | bytes 1310720 | tf_op jit(solution)/shard_map/reduce_scatter | solution.py:283
  245.1 135.2 %copy-start.38 = (f32[4,1,128]{2,1,0:T(1,128)}, f32[4,1,128]{2,1,0:T(1,128)S(1)}, u32[]{:S(2)}) copy-start(f32[4,1,128]{2,1,0:T(1,128)S(1)} %convert_element_type.158) | copy-start | bytes 6148
  250.1 49.9 %copy-start.46 = (f32[4,1,128]{2,1,0:T(1,128)}, f32[4,1,128]{2,1,0:T(1,128)S(1)}, u32[]{:S(2)}) copy-start(f32[4,1,128]{2,1,0:T(1,128)S(1)} %convert_element_type.159) | copy-start | bytes 6148
  255.6 12.0 %copy-start.41 = (f32[24]{0:T(128)}, f32[24]{0:T(128)S(1)}, u32[]{:S(2)}) copy-start(f32[24]{0:T(128)S(1)} %convert_bitcast_fusion.2) | copy-start | bytes 292
  279.2 101.2 %copy-start.27 = (f32[2352]{0:T(1024)}, f32[2352]{0:T(1024)S(1)}, u32[]{:S(2)}) copy-start(f32[2352]{0:T(1024)S(1)} %rsqrt.25) | copy-start | bytes 28228
  279.3 101.0 %copy-start.29 = (f32[2352]{0:T(1024)}, f32[2352]{0:T(1024)S(1)}, u32[]{:S(2)}) copy-start(f32[2352]{0:T(1024)S(1)} %div.52) | copy-start | bytes 28228
  300.0 49.9 %copy-start.31 = (f32[2352]{0:T(1024)S(1)}, f32[2352]{0:T(1024)}, u32[]{:S(2)}) copy-start(f32[2352]{0:T(1024)} %mul.209) | copy-start | bytes 28228
  349.9 18.1 %copy-start.9 = (f32[2352,512]{1,0:T(8,128)S(1)}, f32[2352,512]{1,0:T(8,128)}, u32[]{:S(2)}) copy-start(f32[2352,512]{1,0:T(8,128)} %add.283) | copy-start | bytes 14450692
  349.9 18.1 %copy-start.56 = (bf16[512,2048]{1,0:T(8,128)(2,1)S(1)}, bf16[512,2048]{1,0:T(8,128)(2,1)}, u32[]{:S(2)}) copy-start(bf16[512,2048]{1,0:T(8,128)(2,1)} %all-gather.16.cloned.1.call-done) | copy-start | bytes 6291460
  368.0 12.3 %copy-start.10 = (f32[2352,512]{1,0:T(8,128)S(1)}, f32[2352,512]{1,0:T(8,128)}, u32[]{:S(2)}) copy-start(f32[2352,512]{1,0:T(8,128)} %reshape.409) | copy-start | bytes 14450692
  391.6 25.1 %collective-permute-start.2 = (bf16[24,3,14,512]{3,0,2,1:T(8,128)(2,1)S(1)}, bf16[24,3,14,512]{3,0,2,1:T(8,128)(2,1)S(1)}, u32[]{:S(2)}, u32[]{:S(2)}) collective-permute-start(bf16[24,3,14,512]{3,0,2,1:T(8,128)(2,1)S(1)} %copy.139), channel_id=1, source_target_pairs={{0,16},{16,0},{1,17},{17,1},{2,18},{18,2},{3,19},{19,3},{4,20},{20... | collective-permute-start | bytes 3096584 | tf_op jit(solution)/shard_map/ppermute | solution.py:19
  442.9 13.6 %copy-start.3 = (f32[16,49,49]{1,2,0:T(8,128)S(1)}, f32[16,49,49]{1,2,0:T(8,128)}, u32[]{:S(2)}) copy-start(f32[16,49,49]{1,2,0:T(8,128)} %copy-done.2) | copy-start | bytes 460996
  442.9 13.6 %copy-start.7 = (pred[24,2,49,49]{2,3,1,0:T(8,128)(4,1)S(1)}, pred[24,2,49,49]{2,3,1,0:T(8,128)(4,1)}, u32[]{:S(2)}) copy-start(pred[24,2,49,49]{2,3,1,0:T(8,128)(4,1)} %copy-done.6) | copy-start | bytes 345748
  442.9 13.6 %copy-start.8 = (f32[48,16,49]{2,1,0:T(8,128)S(1)}, f32[48,16,49]{2,1,0:T(8,128)}, u32[]{:S(2)}) copy-start(f32[48,16,49]{2,1,0:T(8,128)} %log_add_fusion) | copy-start | bytes 451588
  456.6 63.9 %slice-start = ((s8[6291456]{0:T(1024)(128)(4,1)}), s8[2097152]{0:T(1024)(128)(4,1)S(1)}, s32[]{:S(2)}) async-start(s8[6291456]{0:T(1024)(128)(4,1)} %bitcast.93), calls=%async_computation.12 | async-start | bytes 4194304
  479.9 40.6 %slice-start.1 = ((s8[6291456]{0:T(1024)(128)(4,1)}), s8[4194304]{0:T(1024)(128)(4,1)S(1)}, s32[]{:S(2)}) async-start(s8[6291456]{0:T(1024)(128)(4,1)} %bitcast.93), calls=%async_computation.13 | async-start | bytes 8388608
  542.7 138.5 %reduce-scatter.5.cloned.1.call-start = ((), (), s32[]{:S(2)}) async-start(), calls=%async_computation.7 | async-start | bytes 3932160 | tf_op jit(solution)/shard_map/reduce_scatter | solution.py:279
  610.1 86.4 %reduce-scatter.11.cloned.1.call-start = ((), (), s32[]{:S(2)}) async-start(), calls=%async_computation.10 | async-start | bytes 5242880 | tf_op jit(solution)/shard_map/reduce_scatter | solution.py:289
  610.2 11.4 %copy-start.28 = (f32[2352]{0:T(1024)S(1)}, f32[2352]{0:T(1024)}, u32[]{:S(2)}) copy-start(f32[2352]{0:T(1024)} %copy-done.27) | copy-start | bytes 28228
  610.2 11.4 %copy-start.30 = (f32[2352]{0:T(1024)S(1)}, f32[2352]{0:T(1024)}, u32[]{:S(2)}) copy-start(f32[2352]{0:T(1024)} %copy-done.29) | copy-start | bytes 28228
  610.2 11.4 %copy-start.39 = (f32[4,1,128]{2,1,0:T(1,128)S(1)}, f32[4,1,128]{2,1,0:T(1,128)}, u32[]{:S(2)}) copy-start(f32[4,1,128]{2,1,0:T(1,128)} %copy-done.38) | copy-start | bytes 6148
  610.2 11.4 %copy-start.47 = (f32[4,1,128]{2,1,0:T(1,128)S(1)}, f32[4,1,128]{2,1,0:T(1,128)}, u32[]{:S(2)}) copy-start(f32[4,1,128]{2,1,0:T(1,128)} %copy-done.46) | copy-start | bytes 6148
  621.3 13.6 %copy-start.22 = (f32[24,7,14]{0,2,1:T(8,128)S(1)}, f32[24,7,14]{0,2,1:T(8,128)}, u32[]{:S(2)}) copy-start(f32[24,7,14]{0,2,1:T(8,128)} %copy-done.21) | copy-start | bytes 28228
  621.3 13.7 %copy-start.19 = (f32[24,7,14]{0,2,1:T(8,128)S(1)}, f32[24,7,14]{0,2,1:T(8,128)}, u32[]{:S(2)}) copy-start(f32[24,7,14]{0,2,1:T(8,128)} %copy-done.18) | copy-start | bytes 28228
  621.3 13.8 %copy-start.58 = (u32[32]{0:T(128)S(1)}, u32[32]{0:T(128)}, u32[]{:S(2)}) copy-start(u32[32]{0:T(128)} %constant.138) | copy-start | bytes 388
  621.3 16.4 %copy-start.54 = (bf16[128]{0:T(256)(128)(2,1)S(1)}, bf16[128]{0:T(256)(128)(2,1)}, u32[]{:S(2)}) copy-start(bf16[128]{0:T(256)(128)(2,1)} %param.33) | copy-start | bytes 772
  621.3 21.8 %copy-start.42 = (f32[24]{0:T(128)S(1)}, f32[24]{0:T(128)}, u32[]{:S(2)}) copy-start(f32[24]{0:T(128)} %copy-done.41) | copy-start | bytes 292
  621.3 122.3 %reduce-scatter.9.cloned.1.call-start = ((), (), s32[]{:S(2)}) async-start(), calls=%async_computation.9 | async-start | bytes 5242880 | tf_op jit(solution)/shard_map/reduce_scatter | solution.py:287
  634.8 241.7 %all-reduce.15.cloned.1.call-start = ((), (), s32[]{:S(2)}) async-start(), calls=%async_computation.11 | async-start | bytes 6291456 | tf_op jit(solution)/shard_map/psum | solution.py:257
  653.3 9.5 %slice-start.2 = ((s8[4816896]{0:T(1024)(128)(4,1)}), s8[622592]{0:T(1024)(128)(4,1)S(1)}, s32[]{:S(2)}) async-start(s8[4816896]{0:T(1024)(128)(4,1)} %bitcast.101), calls=%async_computation.14 | async-start | bytes 1245184
  661.1 89.4 %collective-permute-start.3 = (bf16[24,3,14,512]{3,0,2,1:T(8,128)(2,1)}, bf16[24,3,14,512]{3,0,2,1:T(8,128)(2,1)}, u32[]{:S(2)}, u32[]{:S(2)}) collective-permute-start(bf16[24,3,14,512]{3,0,2,1:T(8,128)(2,1)} %pad_maximum_fusion.4), channel_id=1, source_target_pairs={{0,16},{16,0},{1,17},{17,1},{2,18},{18,2},{3,19},{19,3},{4,20},{20... | collective-permute-start | bytes 3096584 | tf_op jit(solution)/shard_map/ppermute | solution.py:19
  (27 other events, 132.9 us)
Sparse Core Ops, SparseCore 0:
  9.6 22.3 all-gather.13
  33.5 22.6 all-gather.15
  236.7 23.8 all-gather.17
  542.8 26.1 reduce-scatter.6
  610.2 39.2 reduce-scatter.4
  651.9 44.5 reduce-scatter.10
  699.0 44.5 reduce-scatter.8
  747.5 128.8 all-reduce.14
where the time goes:
time: 901 us; the launch traced here: 891 us
  local copies, waits for them, and re-layouts  300 us (33%)
  matrix products  243 us (27%)
  waiting for transfers between devices  123 us (14%)
  blocking collectives  110 us (12%)
  other arithmetic  90.6 us (10%)
  between operations  17.6 us (2%)
    dot_general x1, matrix products, shards(): pre = jnp.dot(normed_two, weight_up, preferred_element_type=f32) + up_bias  49.9 us
    reduce_scatter x1, waiting for transfers between devices, shards(): lax.psum_scatter(s11, 'fsdp', scatter_dimension=0, tiled=True)  47.1 us
    psum x1, blocking collectives, shards(): lax.psum((grad_gain_one, grad_beta_one, grad_wqkv, grad_qbias, grad_vbias...  37.5 us
    psum x1, waiting for transfers between devices, shards(): lax.psum((grad_gain_one, grad_beta_one, grad_wqkv, grad_qbias, grad_vbias...  36.6 us
    unnamed x147, local copies, waits for them, and re-layouts  30.9 us
    reshape x2, local copies, waits for them, and re-layouts, shards(): grad_attended = jnp.dot(grad_proj, weight_out.T, preferred_element_type=f...  25.1 us
    reshape x2, local copies, waits for them, and re-layouts, shards(): ((qkv[:, :D] + query_bias) * scale).astype(bf16)  25 us
    reshape x2, local copies, waits for them, and re-layouts, shards(): (qkv[:, 2 * D:] + value_bias).astype(bf16)  25 us
  transfers between devices with their start and end apart: 12, of which 4 were waited for; matrix products, arithmetic and copies ran while one was open for 51% of the time, Pallas kernels for 0%

commit v1 on v0

--- a/solution.py
+++ b/solution.py
@@ -255,23 +255,26 @@
     final_output = output.reshape(slots, WIN, SIDE, D)
     final_grad = grad_input.reshape(slots, WIN, SIDE, D)
     s01, s02, s03, s04, s05, s06, s07, s08, s09, s10, s11, s12, s13, s14 = lax.psum(
-        (
-            grad_gain_one,
-            grad_beta_one,
-            grad_wqkv,
-            grad_qbias,
-            grad_vbias,
-            grad_table,
-            grad_wout,
-            grad_projb,
-            grad_gain_two,
-            grad_beta_two,
-            grad_up,
-            grad_upb,
-            grad_down,
-            grad_downb,
+        lax.psum(
+            (
+                grad_gain_one,
+                grad_beta_one,
+                grad_wqkv,
+                grad_qbias,
+                grad_vbias,
+                grad_table,
+                grad_wout,
+                grad_projb,
+                grad_gain_two,
+                grad_beta_two,
+                grad_up,
+                grad_upb,
+                grad_down,
+                grad_downb,
+            ),
+            "img",
         ),
-        ("band", "img"),
+        "band",
     )
     r01, r02, r03, r04, r05, r06, r07, r08, r09, r10, r11, r12, r13, r14 = (
         lax.psum_scatter(s01, "fsdp", scatter_dimension=0, tiled=True),

time: 901 us -> 979 us (1.087)
  waiting for transfers between devices: 123 us -> 212 us
  blocking collectives: 110 us -> 99.1 us
    psum x1, waiting for transfers between devices: 36.6 us -> 86.7 us  [shards(): lax.psum((grad_gain_one, grad_beta_one, grad_wqkv, grad_qbias, grad_vbias...]
    reduce_scatter x1, waiting for transfers between devices: 15.3 us -> 47 us  [shards(): lax.psum_scatter(s13, 'fsdp', scatter_dimension=0, tiled=True)]
    psum x1, blocking collectives: 37.5 us -> 16.9 us  [shards(): lax.psum((grad_gain_one, grad_beta_one, grad_wqkv, grad_qbias, grad_vbias...]
  transfers between devices with their start and end apart: 12 -> 13, of which waited for: 4 -> 6; matrix products, arithmetic and copies ran while one was open for 51% -> 47% of each run, Pallas kernels for 0% -> 0%
where the time goes in v1:
time: 979 us; the launch traced here: 969 us
  local copies, waits for them, and re-layouts  301 us (31%)
  matrix products  243 us (25%)
  waiting for transfers between devices  212 us (22%)
  blocking collectives  99.1 us (10%)
  other arithmetic  90.7 us (9%)
  between operations  17.3 us (2%)
    psum x1, waiting for transfers between devices, shards(): lax.psum((grad_gain_one, grad_beta_one, grad_wqkv, grad_qbias, grad_vbias...  86.7 us
    dot_general x1, matrix products, shards(): pre = jnp.dot(normed_two, weight_up, preferred_element_type=f32) + up_bias  49.9 us
    reduce_scatter x1, waiting for transfers between devices, shards(): lax.psum_scatter(s11, 'fsdp', scatter_dimension=0, tiled=True)  47.1 us
    reduce_scatter x1, waiting for transfers between devices, shards(): lax.psum_scatter(s13, 'fsdp', scatter_dimension=0, tiled=True)  47 us
    unnamed x147, local copies, waits for them, and re-layouts  31.3 us
    reshape x2, local copies, waits for them, and re-layouts, shards(): grad_attended = jnp.dot(grad_proj, weight_out.T, preferred_element_type=f...  25.1 us
    reshape x2, local copies, waits for them, and re-layouts, shards(): ((qkv[:, :D] + query_bias) * scale).astype(bf16)  25 us
    reshape x2, local copies, waits for them, and re-layouts, shards(): (qkv[:, 2 * D:] + value_bias).astype(bf16)  25 us
  transfers between devices with their start and end apart: 13, of which 6 were waited for; matrix products, arithmetic and copies ran while one was open for 47% of the time, Pallas kernels for 0%

profile of v1, /device:TPU:0, one launch (start us, length us, event | category | flops | bytes accessed | tf_op | source)
XLA Modules:
  0.0 969.3 jit_solution(13817478064361988633)
XLA Ops:
  8.0 6.2 all-gather
  54.8 7.9 all_gather.48
  84.7 11.5 %reshape.462 = bf16[48,49,16,32]{3,2,1,0:T(8,128)(2,1)} reshape(bf16[2352,512]{1,0:T(8,128)(2,1)} %get-tuple-element.131) | data formatting | bytes 4816896 | tf_op jit(solution)/shard_map/reshape | solution.py:171
  96.2 13.5 %copy.127 = bf16[48,49,16,32]{1,3,2,0:T(8,128)(2,1)} copy(bf16[48,49,16,32]{3,2,1,0:T(8,128)(2,1)} %reshape.462) | data formatting | bytes 4816896 | tf_op jit(solution)/shard_map/reshape | solution.py:171
  109.8 11.5 %reshape.463 = bf16[48,49,16,32]{3,2,1,0:T(8,128)(2,1)} reshape(bf16[2352,512]{1,0:T(8,128)(2,1)} %slice.113) | data formatting | bytes 4816896 | tf_op jit(solution)/shard_map/reshape | solution.py:172
  121.3 13.5 %copy.128 = bf16[48,49,16,32]{1,3,2,0:T(8,128)(2,1)} copy(bf16[48,49,16,32]{3,2,1,0:T(8,128)(2,1)} %reshape.463) | data formatting | bytes 4816896 | tf_op jit(solution)/shard_map/reshape | solution.py:172
  134.9 13.4 %fusion.15 = (f32[48,16,49]{2,1,0:T(8,128)S(1)}, f32[48,16,49,49]{2,3,1,0:T(8,128)}) fusion(f32[16,49,49]{1,2,0:T(8,128)S(1)} %copy.129, pred[48,49,49]{1,2,0:T(8,128)(4,1)S(1)} %bitcast.95, bf16[48,49,16,32]{1,3,2,0:T(8,128)(2,1)} %copy.127, bf16[48,49,16,32]{1,3,2,0:T(8,128)(2,1)} %copy.128), kind=kOutput, calls=%fused_computation.30 | convolution fusion | flops 123508224 | bytes 12612208 | tf_op jit(solution)/shard_map/wqhd,wkhd->whqk/dot_general | solution.py:86
  148.3 13.4 %exponential_reduce_fusion = f32[48,16,49]{2,1,0:T(8,128)S(1)} fusion(f32[48,16,49,49]{2,3,1,0:T(8,128)} %get-tuple-element.136, f32[48,16,49]{2,1,0:T(8,128)S(1)} %get-tuple-element.135, f32[16,49,49]{1,2,0:T(8,128)S(1)} %copy.129, pred[48,49,49]{1,2,0:T(8,128)(4,1)S(1)} %bitcast.96), kind=kLoop, calls=%fused_computation.5 | loop fusion | flops 7338240 | bytes 7945840 | tf_op jit(solution)/shard_map/reduce_sum | solution.py:176
  162.5 11.5 %reshape.461 = bf16[48,49,16,32]{3,2,1,0:T(8,128)(2,1)} reshape(bf16[2352,512]{1,0:T(8,128)(2,1)} %get-tuple-element.132) | data formatting | bytes 4816896 | tf_op jit(solution)/shard_map/reshape | solution.py:173
  174.0 13.5 %copy.130 = bf16[48,49,16,32]{1,3,2,0:T(8,128)(2,1)} copy(bf16[48,49,16,32]{3,2,1,0:T(8,128)(2,1)} %reshape.461) | data formatting | bytes 4816896 | tf_op jit(solution)/shard_map/reshape | solution.py:173
  187.6 14.4 %convert_bitcast_fusion.1 = bf16[48,49,16,32]{1,3,2,0:T(8,128)(2,1)} fusion(bf16[48,49,16,32]{1,3,2,0:T(8,128)(2,1)} %copy.130, f32[48,16,49,49]{2,3,1,0:T(8,128)} %get-tuple-element.136, f32[48,16,49]{2,1,0:T(8,128)} %log_add_fusion, f32[16,49,49]{1,2,0:T(8,128)S(1)} %copy.129, pred[48,49,49]{1,2,0:T(8,128)(4,1)S(1)} %bitcast.97), kind=kOutput, calls=%fused_computation.38 | convolution fusion | flops 126594048 | bytes 12612208 | tf_op jit(solution)/shard_map/whqk,wkhd->wqhd/dot_general | solution.py:179
  201.9 9.5 copy.132
  211.5 9.2 reshape.405
  261.2 6.3 reshape.409
  267.6 6.3 reshape.399
  286.5 6.4 reshape.420
  292.9 7.1 add.311
  300.0 49.9 %fusion.2 = (bf16[2352,2048]{1,0:T(8,128)(2,1)}, f32[2352,2048]{1,0:T(8,128)}) fusion(f32[2048]{0:T(1024)S(1)} %bitcast.122, bf16[512,2048]{1,0:T(8,128)(2,1)} %all-gather.16.cloned.1.call-done, f32[2352,512]{1,0:T(8,128)} %add.311, f32[512]{0:T(512)S(1)} %bitcast.125, f32[512]{0:T(512)S(1)} %bitcast.115, f32[2352]{0:T(1024)S(1)} %rsqrt.25, f32[2352]{0:T(1024)S(1)} %div.52), kind=kOutput, calls=%fused_computation.9 | convolution fusion | flops 5256437760 | bytes 35846528 | tf_op jit(solution)/shard_map/dot_general | solution.py:190
  349.9 18.1 %fusion.50 = (f32[2048]{0:T(1024)}, bf16[2352,2048]{1,0:T(8,128)(2,1)}) fusion(f32[2352,2048]{1,0:T(8,128)} %get-tuple-element.138, f32[2048]{0:T(1024)S(1)} %bitcast.123, bf16[2048,512]{1,0:T(8,128)(2,1)} %all-gather.18.cloned.1.call-done, f32[2352,512]{1,0:T(8,128)} %reshape.409, f32[2352]{0:T(1024)S(1)} %copy-done.31), kind=kOutput, calls=%fused_computation.130 | convolution fusion | flops 4992710656 | bytes 35841216 | tf_op jit(solution)/shard_map/dot_general | solution.py:199
  368.0 12.3 %multiply_reduce_fusion.3 = (f32[512]{0:T(512)}, f32[2352]{0:T(1024)S(1)}, f32[2352]{0:T(1024)S(1)}, f32[512]{0:T(512)}, f32[2352,512]{1,0:T(8,128)S(1)}) fusion(f32[2352,512]{1,0:T(8,128)S(1)} %copy-done.9, f32[2352]{0:T(1024)S(1)} %rsqrt.25, f32[2352]{0:T(1024)S(1)} %div.52, f32[512]{0:T(512)S(1)} %bitcast.116, bf16[512,2048]{1,0:T(8,128)(2,1)S(1)} %copy-done.56, ...), kind=kOutput, calls=%fused_computation.51 | convolution fusion | flops 4943333376 | bytes 21408512 | tf_op jit(solution)/shard_map/dot_general | solution.py:203
  393.5 23.3 %collective-permute-done.2 = bf16[24,3,14,512]{3,0,2,1:T(8,128)(2,1)S(1)} collective-permute-done((bf16[24,3,14,512]{3,0,2,1:T(8,128)(2,1)S(1)}, bf16[24,3,14,512]{3,0,2,1:T(8,128)(2,1)S(1)}, u32[]{:S(2)}, u32[]{:S(2)}) %collective-permute-start.2) | collective-permute-done | bytes 1032224 | tf_op jit(solution)/shard_map/ppermute | solution.py:19
  431.4 11.5 %reshape.464 = bf16[48,49,16,32]{3,2,1,0:T(8,128)(2,1)} reshape(bf16[2352,512]{1,0:T(8,128)(2,1)} %convolution_convert_fusion.1) | data formatting | bytes 4816896 | tf_op jit(solution)/shard_map/reshape | solution.py:217
  442.9 13.6 %copy.144 = bf16[48,49,16,32]{1,3,2,0:T(8,128)(2,1)} copy(bf16[48,49,16,32]{3,2,1,0:T(8,128)(2,1)} %reshape.464) | data formatting | bytes 4816896 | tf_op jit(solution)/shard_map/reshape | solution.py:217
  456.6 23.3 %multiply_reduce_fusion = (f32[48,16,49]{2,1,0:T(8,128)S(1)}, f32[48,16,49,49]{2,3,1,0:T(8,128)}) fusion(f32[48,16,49,49]{2,3,1,0:T(8,128)} %get-tuple-element.136, f32[48,16,49]{2,1,0:T(8,128)S(1)} %copy-done.8, f32[16,49,49]{1,2,0:T(8,128)S(1)} %copy-done.3, pred[48,49,49]{1,2,0:T(8,128)(4,1)S(1)} %bitcast.98, bf16[48,49,16,32]{1,3,2,0:T(8,128)(2,1)} %copy.144, ...), kind=kOutput, calls=%fused_computation.3 | convolution fusion | flops 127196160 | bytes 20138608 | tf_op jit(solution)/shard_map/wqhd,wkhd->whqk/dot_general | solution.py:220
  479.9 19.4 %bitcast_convert_fusion = (bf16[48,49,16,32]{1,3,2,0:T(8,128)(2,1)}, f32[48,16,32,49]{3,2,1,0:T(8,128)}) fusion(bf16[48,49,16,32]{1,3,2,0:T(8,128)(2,1)} %copy.144, f32[48,16,49,49]{2,3,1,0:T(8,128)} %get-tuple-element.136, f32[48,16,49]{2,1,0:T(8,128)S(1)} %copy-done.8, f32[16,49,49]{1,2,0:T(8,128)S(1)} %copy-done.3, pred[48,49,49]{1,2,0:T(8,128)(4,1)S(1)} %bitcast.99), kind=kOutput, calls=%fused_computation.32 | convolution fusion | flops 126594048 | bytes 17429104 | tf_op jit(solution)/shard_map/whqk,wqhd->wkhd/dot_general | solution.py:237
  499.2 21.2 %fusion.48 = (f32[16,49,49]{1,2,0:T(8,128)}, bf16[48,16,49,49]{2,3,1,0:T(8,128)(2,1)}) fusion(f32[48,16,49,49]{2,3,1,0:T(8,128)} %get-tuple-element.141, f32[48,16,49]{2,1,0:T(8,128)S(1)} %get-tuple-element.140, f32[48,16,49]{2,1,0:T(8,128)S(1)} %copy-done.8, f32[48,16,49,49]{2,3,1,0:T(8,128)} %get-tuple-element.136, f32[16,49,49]{1,2,0:T(8,128)S(1)} %copy-done.3, ...), kind=kLoop, calls=%fused_computation.129 | loop fusion | flops 12869360 | bytes 19163312 | tf_op jit(solution)/shard_map/reduce_sum | solution.py:223
  520.4 10.4 %convert_bitcast_fusion = bf16[48,49,16,32]{1,3,2,0:T(8,128)(2,1)} fusion(bf16[48,49,16,32]{1,3,2,0:T(8,128)(2,1)S(1)} %bitcast.94, bf16[48,16,49,49]{2,3,1,0:T(8,128)(2,1)} %get-tuple-element.129), kind=kOutput, calls=%fused_computation.37 | convolution fusion | flops 119218176 | bytes 8504832 | tf_op jit(solution)/shard_map/whqk,wqhd->wkhd/dot_general | solution.py:234
  530.8 11.9 %multiply_reduce_fusion.1 = (f32[16,32]{1,0:T(8,128)S(1)}, bf16[48,49,16,32]{1,3,2,0:T(8,128)(2,1)}) fusion(bf16[48,49,16,32]{1,3,2,0:T(8,128)(2,1)} %copy.128, bf16[48,16,49,49]{2,3,1,0:T(8,128)(2,1)} %get-tuple-element.129), kind=kOutput, calls=%fused_computation.33 | convolution fusion | flops 121626112 | bytes 8506880 | tf_op jit(solution)/shard_map/whqk,wkhd->wqhd/dot_general | solution.py:229
  542.8 9.6 copy.151
  552.3 8.5 reshape.414
  560.8 9.6 copy.154
  570.4 9.2 reshape.415
  579.6 9.4 copy.148
  589.0 9.3 mul.250
  610.2 11.0 %fusion.42 = f32[2048,512]{1,0:T(8,128)} fusion(bf16[2352,2048]{1,0:T(8,128)(2,1)} %get-tuple-element.137, f32[2352,512]{1,0:T(8,128)} %reshape.409, f32[2352]{0:T(1024)S(1)} %copy-done.32), kind=kOutput, calls=%fused_computation.125 | convolution fusion | flops 4934909952 | bytes 18654400 | tf_op jit(solution)/shard_map/dot_general | solution.py:197
  621.6 13.1 %fusion.25 = f32[512,2048]{1,0:T(8,128)} fusion(bf16[2352,2048]{1,0:T(8,128)(2,1)} %get-tuple-element.145, f32[2352,512]{1,0:T(8,128)} %add.311, f32[512]{0:T(512)S(1)} %bitcast.126, f32[512]{0:T(512)S(1)} %bitcast.118, f32[2352]{0:T(1024)S(1)} %copy-done.28, f32[2352]{0:T(1024)S(1)} %copy-done.30), kind=kOutput, calls=%fused_computation.57 | convolution fusion | flops 4938522624 | bytes 18667904 | tf_op jit(solution)/shard_map/dot_general | solution.py:202
  649.5 47.0 %reduce-scatter.11.cloned.1.call-done = f32[512,512]{1,0:T(8,128)} async-done(((f32[2048,512]{1,0:T(8,128)}), f32[512,512]{1,0:T(8,128)}) %reduce-scatter.11.cloned.1.call-update) | async-done | bytes 1048592 | tf_op jit(solution)/shard_map/reduce_scatter | solution.py:292
  696.5 47.1 %reduce-scatter.9.cloned.1.call-done = f32[128,2048]{1,0:T(8,128)} async-done(((f32[512,2048]{1,0:T(8,128)}), f32[128,2048]{1,0:T(8,128)}) %reduce-scatter.9.cloned.1.call-update) | async-done | bytes 1048592 | tf_op jit(solution)/shard_map/reduce_scatter | solution.py:290
  743.7 9.2 convolution_convert_fusion
  762.2 10.6 %multiply_convert_fusion.1 = bf16[2352,512]{1,0:T(8,128)(2,1)} fusion(f32[2352,512]{1,0:T(8,128)S(1)} %bitcast.102, bf16[2352,2048]{1,0:T(8,128)(2,1)} %get-tuple-element.137, bf16[2048,512]{1,0:T(8,128)(2,1)S(1)} %copy-done.55, f32[512]{0:T(512)S(1)} %bitcast.128, f32[2352]{0:T(1024)S(1)} %copy-done.32), kind=kOutput, calls=%fused_computation.61 | convolution fusion | flops 4937318400 | bytes 18967744 | tf_op jit(solution)/shard_map/dot_general | solution.py:192
  780.7 86.7 %all-reduce.18.cloned.1.call-done = (f32[128,1536]{1,0:T(8,128)}, f32[128,512]{1,0:T(8,128)}, f32[128,2048]{1,0:T(8,128)}, f32[512,512]{1,0:T(8,128)}) async-done(((f32[128,1536]{1,0:T(8,128)}, f32[128,512]{1,0:T(8,128)}, f32[128,2048]{1,0:T(8,128)}, f32[512,512]{1,0:T(8,128)}), (f32[128,1536]{1,0:T(8,128)}, f32[128,512]{1,0:T(8,128)}, f32[128,2048]{1,0:T(8,128)}, ...) | async-done | bytes 3145744 | tf_op jit(solution)/shard_map/psum | solution.py:258
  879.9 12.3 %all-reduce.10 = (f32[512]{0:T(512)S(1)}, f32[512]{0:T(512)S(1)}, f32[512]{0:T(512)S(1)}, f32[512]{0:T(512)S(1)}, f32[16,169]{1,0:T(8,128)S(1)}, /*index=5*/f32[...) all-reduce(f32[512]{0:T(512)S(1)} %get-tuple-element.82, ...), channel_id=2, replica_groups=mesh['band'=2,'img'=4,'fsdp'=4] {'fsdp'}, use_global_device_ids=true, to_apply=%region_14.15.clone | all-reduce | flops 8848 | bytes 70784
  898.3 6.4 reshape.421
  904.7 8.0 multiply_add_fusion
  912.6 6.3 reshape.418
  918.9 8.3 copy.162
  927.3 16.9 %all-reduce.11 = (f32[128]{0:T(128)S(1)}, f32[128]{0:T(128)S(1)}, f32[128]{0:T(128)S(1)}, f32[128]{0:T(128)S(1)}, f32[4,169]{1,0:T(4,128)S(1)}, /*index=5*/f32[1...) all-reduce(f32[128]{0:T(128)S(1)} %dynamic-slice.1, ...), channel_id=1, replica_groups=mesh['band'=2,'img'=4,'fsdp'=4] {'img'}, use_global_device_ids=true, to_apply=%region_12.13 | all-reduce | flops 2212 | bytes 17696 | tf_op jit(solution)/shard_map/psum | solution.py:258
  944.1 9.1 all-reduce.13
  (288 shorter events, 214.5 us)
Async XLA Ops:
  7.2 17.4 %copy-start = (bf16[24,7,14,512]{3,0,2,1:T(8,128)(2,1)S(1)}, bf16[24,7,14,512]{3,0,2,1:T(8,128)(2,1)}, u32[]{:S(2)}) copy-start(bf16[24,7,14,512]{3,0,2,1:T(8,128)(2,1)} %param.17) | copy-start | bytes 7225348
  7.2 65.9 %all-gather.14.cloned.1.call-start = ((), (), s32[]{:S(2)}) async-start(), calls=%async_computation.4 | async-start | bytes 1966080 | tf_op jit(solution)/shard_map/all_gather | solution.py:132
  7.9 292.1 %all-gather.16.cloned.1.call-start = ((), (), s32[]{:S(2)}) async-start(), calls=%async_computation.5 | async-start | bytes 2621440 | tf_op jit(solution)/shard_map/all_gather | solution.py:140
  14.2 11.5 %copy-start.33 = (f32[4,1,128]{2,1,0:T(1,128)}, f32[4,1,128]{2,1,0:T(1,128)S(1)}, u32[]{:S(2)}) copy-start(f32[4,1,128]{2,1,0:T(1,128)S(1)} %convert_element_type.153) | copy-start | bytes 6148
  24.6 13.1 %copy-start.50 = (bf16[128]{0:T(256)(128)(2,1)S(1)}, bf16[128]{0:T(256)(128)(2,1)}, u32[]{:S(2)}) copy-start(bf16[128]{0:T(256)(128)(2,1)} %param.24) | copy-start | bytes 772
  24.7 18.1 %copy-start.51 = (bf16[128]{0:T(256)(128)(2,1)S(1)}, bf16[128]{0:T(256)(128)(2,1)}, u32[]{:S(2)}) copy-start(bf16[128]{0:T(256)(128)(2,1)} %param.27) | copy-start | bytes 772
  24.7 23.3 %copy-start.43 = (bf16[4,169]{1,0:T(4,128)(2,1)S(1)}, bf16[4,169]{1,0:T(4,128)(2,1)}, u32[]{:S(2)}) copy-start(bf16[4,169]{1,0:T(4,128)(2,1)} %param.25) | copy-start | bytes 4060
  27.2 27.6 %copy-start.26 = (bf16[128,512]{1,0:T(8,128)(2,1)S(1)}, bf16[128,512]{1,0:T(8,128)(2,1)}, u32[]{:S(2)}) copy-start(bf16[128,512]{1,0:T(8,128)(2,1)} %param.26) | copy-start | bytes 393220
  28.2 34.5 %collective-permute-start = (bf16[24,3,14,512]{3,0,2,1:T(8,128)(2,1)}, bf16[24,3,14,512]{3,0,2,1:T(8,128)(2,1)}, u32[]{:S(2)}, u32[]{:S(2)}) collective-permute-start(bf16[24,3,14,512]{3,0,2,1:T(8,128)(2,1)} %slice.82), channel_id=1, source_target_pairs={{0,16},{16,0},{1,17},{17,1},{2,18},{18,2},{3,19},{19,3},{4,20},{20... | collective-permute-start | bytes 3096584 | tf_op jit(solution)/shard_map/ppermute | solution.py:19
  30.0 319.9 %all-gather.18.cloned.1.call-start = ((), (), s32[]{:S(2)}) async-start(), calls=%async_computation.6 | async-start | bytes 2621440 | tf_op jit(solution)/shard_map/all_gather | solution.py:142
  54.7 132.9 %copy-start.2 = (f32[16,49,49]{1,2,0:T(8,128)}, f32[16,49,49]{1,2,0:T(8,128)S(1)}, u32[]{:S(2)}) copy-start(f32[16,49,49]{1,2,0:T(8,128)S(1)} %copy.129) | copy-start | bytes 460996
  54.7 9.6 copy-start.12
  134.9 52.7 %copy-start.6 = (pred[24,2,49,49]{2,3,1,0:T(8,128)(4,1)}, pred[24,2,49,49]{2,3,1,0:T(8,128)(4,1)S(1)}, u32[]{:S(2)}) copy-start(pred[24,2,49,49]{2,3,1,0:T(8,128)(4,1)S(1)} %broadcast_in_dim.38) | copy-start | bytes 345748
  236.1 14.0 %copy-start.48 = (bf16[512]{0:T(512)(128)(2,1)S(1)}, bf16[512]{0:T(512)(128)(2,1)}, u32[]{:S(2)}) copy-start(bf16[512]{0:T(512)(128)(2,1)} %param.31) | copy-start | bytes 3076
  236.1 19.5 %copy-start.57 = (s32[1,24]{1,0:T(1,128)S(1)}, s32[1,24]{1,0:T(1,128)}, u32[]{:S(2)}) copy-start(s32[1,24]{1,0:T(1,128)} %param.18) | copy-start | bytes 292
  236.1 37.8 %collective-permute-start.1 = (bf16[24,3,14,512]{3,0,2,1:T(8,128)(2,1)}, bf16[24,3,14,512]{3,0,2,1:T(8,128)(2,1)}, u32[]{:S(2)}, u32[]{:S(2)}) collective-permute-start(bf16[24,3,14,512]{3,0,2,1:T(8,128)(2,1)} %pad_maximum_fusion.5), channel_id=1, source_target_pairs={{0,16},{16,0},{1,17},{17,1},{2,18},{18,2},{3,19},{19,3},{4,20},{20... | collective-permute-start | bytes 3096584 | tf_op jit(solution)/shard_map/ppermute | solution.py:19
  236.6 407.4 %reduce-scatter.7.cloned.1.call-start = ((), (), s32[]{:S(2)}) async-start(), calls=%async_computation.8 | async-start | bytes 1310720 | tf_op jit(solution)/shard_map/reduce_scatter | solution.py:286
  245.1 135.2 %copy-start.38 = (f32[4,1,128]{2,1,0:T(1,128)}, f32[4,1,128]{2,1,0:T(1,128)S(1)}, u32[]{:S(2)}) copy-start(f32[4,1,128]{2,1,0:T(1,128)S(1)} %convert_element_type.158) | copy-start | bytes 6148
  250.1 49.9 %copy-start.46 = (f32[4,1,128]{2,1,0:T(1,128)}, f32[4,1,128]{2,1,0:T(1,128)S(1)}, u32[]{:S(2)}) copy-start(f32[4,1,128]{2,1,0:T(1,128)S(1)} %convert_element_type.159) | copy-start | bytes 6148
  255.6 12.0 %copy-start.41 = (f32[24]{0:T(128)}, f32[24]{0:T(128)S(1)}, u32[]{:S(2)}) copy-start(f32[24]{0:T(128)S(1)} %convert_bitcast_fusion.2) | copy-start | bytes 292
  279.2 101.2 %copy-start.27 = (f32[2352]{0:T(1024)}, f32[2352]{0:T(1024)S(1)}, u32[]{:S(2)}) copy-start(f32[2352]{0:T(1024)S(1)} %rsqrt.25) | copy-start | bytes 28228
  279.3 101.0 %copy-start.29 = (f32[2352]{0:T(1024)}, f32[2352]{0:T(1024)S(1)}, u32[]{:S(2)}) copy-start(f32[2352]{0:T(1024)S(1)} %div.52) | copy-start | bytes 28228
  300.0 49.9 %copy-start.31 = (f32[2352]{0:T(1024)S(1)}, f32[2352]{0:T(1024)}, u32[]{:S(2)}) copy-start(f32[2352]{0:T(1024)} %mul.209) | copy-start | bytes 28228
  349.9 18.1 %copy-start.9 = (f32[2352,512]{1,0:T(8,128)S(1)}, f32[2352,512]{1,0:T(8,128)}, u32[]{:S(2)}) copy-start(f32[2352,512]{1,0:T(8,128)} %add.311) | copy-start | bytes 14450692
  349.9 18.1 %copy-start.56 = (bf16[512,2048]{1,0:T(8,128)(2,1)S(1)}, bf16[512,2048]{1,0:T(8,128)(2,1)}, u32[]{:S(2)}) copy-start(bf16[512,2048]{1,0:T(8,128)(2,1)} %all-gather.16.cloned.1.call-done) | copy-start | bytes 6291460
  368.0 12.3 %copy-start.10 = (f32[2352,512]{1,0:T(8,128)S(1)}, f32[2352,512]{1,0:T(8,128)}, u32[]{:S(2)}) copy-start(f32[2352,512]{1,0:T(8,128)} %reshape.409) | copy-start | bytes 14450692
  391.6 25.1 %collective-permute-start.2 = (bf16[24,3,14,512]{3,0,2,1:T(8,128)(2,1)S(1)}, bf16[24,3,14,512]{3,0,2,1:T(8,128)(2,1)S(1)}, u32[]{:S(2)}, u32[]{:S(2)}) collective-permute-start(bf16[24,3,14,512]{3,0,2,1:T(8,128)(2,1)S(1)} %copy.139), channel_id=1, source_target_pairs={{0,16},{16,0},{1,17},{17,1},{2,18},{18,2},{3,19},{19,3},{4,20},{20... | collective-permute-start | bytes 3096584 | tf_op jit(solution)/shard_map/ppermute | solution.py:19
  442.9 13.6 %copy-start.3 = (f32[16,49,49]{1,2,0:T(8,128)S(1)}, f32[16,49,49]{1,2,0:T(8,128)}, u32[]{:S(2)}) copy-start(f32[16,49,49]{1,2,0:T(8,128)} %copy-done.2) | copy-start | bytes 460996
  442.9 13.6 %copy-start.7 = (pred[24,2,49,49]{2,3,1,0:T(8,128)(4,1)S(1)}, pred[24,2,49,49]{2,3,1,0:T(8,128)(4,1)}, u32[]{:S(2)}) copy-start(pred[24,2,49,49]{2,3,1,0:T(8,128)(4,1)} %copy-done.6) | copy-start | bytes 345748
  442.9 13.6 %copy-start.8 = (f32[48,16,49]{2,1,0:T(8,128)S(1)}, f32[48,16,49]{2,1,0:T(8,128)}, u32[]{:S(2)}) copy-start(f32[48,16,49]{2,1,0:T(8,128)} %log_add_fusion) | copy-start | bytes 451588
  456.6 63.9 %slice-start = ((s8[6291456]{0:T(1024)(128)(4,1)}), s8[2097152]{0:T(1024)(128)(4,1)S(1)}, s32[]{:S(2)}) async-start(s8[6291456]{0:T(1024)(128)(4,1)} %bitcast.93), calls=%async_computation.13 | async-start | bytes 4194304
  479.9 40.6 %slice-start.1 = ((s8[6291456]{0:T(1024)(128)(4,1)}), s8[4194304]{0:T(1024)(128)(4,1)S(1)}, s32[]{:S(2)}) async-start(s8[6291456]{0:T(1024)(128)(4,1)} %bitcast.93), calls=%async_computation.14 | async-start | bytes 8388608
  542.7 106.8 %reduce-scatter.5.cloned.1.call-start = ((), (), s32[]{:S(2)}) async-start(), calls=%async_computation.7 | async-start | bytes 3932160 | tf_op jit(solution)/shard_map/reduce_scatter | solution.py:282
  610.1 86.4 %reduce-scatter.11.cloned.1.call-start = ((), (), s32[]{:S(2)}) async-start(), calls=%async_computation.10 | async-start | bytes 5242880 | tf_op jit(solution)/shard_map/reduce_scatter | solution.py:292
  610.2 11.4 %copy-start.28 = (f32[2352]{0:T(1024)S(1)}, f32[2352]{0:T(1024)}, u32[]{:S(2)}) copy-start(f32[2352]{0:T(1024)} %copy-done.27) | copy-start | bytes 28228
  610.2 11.4 %copy-start.30 = (f32[2352]{0:T(1024)S(1)}, f32[2352]{0:T(1024)}, u32[]{:S(2)}) copy-start(f32[2352]{0:T(1024)} %copy-done.29) | copy-start | bytes 28228
  610.2 11.4 %copy-start.39 = (f32[4,1,128]{2,1,0:T(1,128)S(1)}, f32[4,1,128]{2,1,0:T(1,128)}, u32[]{:S(2)}) copy-start(f32[4,1,128]{2,1,0:T(1,128)} %copy-done.38) | copy-start | bytes 6148
  610.2 11.4 %copy-start.47 = (f32[4,1,128]{2,1,0:T(1,128)S(1)}, f32[4,1,128]{2,1,0:T(1,128)}, u32[]{:S(2)}) copy-start(f32[4,1,128]{2,1,0:T(1,128)} %copy-done.46) | copy-start | bytes 6148
  621.3 13.6 %copy-start.22 = (f32[24,7,14]{0,2,1:T(8,128)S(1)}, f32[24,7,14]{0,2,1:T(8,128)}, u32[]{:S(2)}) copy-start(f32[24,7,14]{0,2,1:T(8,128)} %copy-done.21) | copy-start | bytes 28228
  621.3 13.7 %copy-start.19 = (f32[24,7,14]{0,2,1:T(8,128)S(1)}, f32[24,7,14]{0,2,1:T(8,128)}, u32[]{:S(2)}) copy-start(f32[24,7,14]{0,2,1:T(8,128)} %copy-done.18) | copy-start | bytes 28228
  621.3 13.8 %copy-start.58 = (u32[32]{0:T(128)S(1)}, u32[32]{0:T(128)}, u32[]{:S(2)}) copy-start(u32[32]{0:T(128)} %constant.138) | copy-start | bytes 388
  621.3 16.4 %copy-start.54 = (bf16[128]{0:T(256)(128)(2,1)S(1)}, bf16[128]{0:T(256)(128)(2,1)}, u32[]{:S(2)}) copy-start(bf16[128]{0:T(256)(128)(2,1)} %param.33) | copy-start | bytes 772
  621.3 21.8 %copy-start.42 = (f32[24]{0:T(128)S(1)}, f32[24]{0:T(128)}, u32[]{:S(2)}) copy-start(f32[24]{0:T(128)} %copy-done.41) | copy-start | bytes 292
  621.3 122.3 %reduce-scatter.9.cloned.1.call-start = ((), (), s32[]{:S(2)}) async-start(), calls=%async_computation.9 | async-start | bytes 5242880 | tf_op jit(solution)/shard_map/reduce_scatter | solution.py:290
  634.8 232.6 %all-reduce.18.cloned.1.call-start = ((), (), s32[]{:S(2)}) async-start(), calls=%async_computation.11 | async-start | bytes 6291456 | tf_op jit(solution)/shard_map/psum | solution.py:258
  743.7 211.5 %all-reduce.20.cloned.1.call-start = ((), (), s32[]{:S(2)}) async-start(), calls=%async_computation.12 | async-start | bytes 6291456 | tf_op jit(solution)/shard_map/psum | solution.py:257
  752.9 9.3 slice-start.2
  760.7 113.6 %collective-permute-start.3 = (bf16[24,3,14,512]{3,0,2,1:T(8,128)(2,1)}, bf16[24,3,14,512]{3,0,2,1:T(8,128)(2,1)}, u32[]{:S(2)}, u32[]{:S(2)}) collective-permute-start(bf16[24,3,14,512]{3,0,2,1:T(8,128)(2,1)} %pad_maximum_fusion.4), channel_id=1, source_target_pairs={{0,16},{16,0},{1,17},{17,1},{2,18},{18,2},{3,19},{19,3},{4,20},{20... | collective-permute-start | bytes 3096584 | tf_op jit(solution)/shard_map/ppermute | solution.py:19
  (28 other events, 142.5 us)
Sparse Core Ops, SparseCore 0:
  9.6 22.3 all-gather.13
  33.5 22.6 all-gather.15
  236.7 23.8 all-gather.17
  542.8 26.1 reduce-scatter.6
  610.2 39.2 reduce-scatter.4
  651.9 44.5 reduce-scatter.10
  699.0 44.5 reduce-scatter.8
  746.2 121.0 all-reduce.17
  869.8 85.2 all-reduce.19
